TPU v7x, 32 devices: a whole 2x2x4 slice. The times are simulated.
32 devices in a mesh: gx: 8 (over y, x, core), gy: 4 (over z).
Axes of the slice: x: 2, y: 2, z: 4, core: 2. Of those that a mesh axis runs over, the one named last changes fastest.
Arguments:
- adjoint_source: float32 [4, 64, 256, 512], P(None, 'gx', 'gy'), may hold values from -40 to 40, as said below
- conductivity: float32 [64, 256, 512], P('gx', 'gy'), may hold values from 0.1 to 10
- electrodes: int32 [4], replicated, may hold values from 0 to 16383
Outputs:
- solution_field: float32 [4, 64, 256, 512], P(None, 'gx', 'gy')
- residual: float32 [4, 64, 256, 512], P(None, 'gx', 'gy')
Inputs may be any that keep to these rules, and one draw needn't show every extreme that they name: `electrodes`: each entry is a surface cell index, its first coordinate times 256 plus its second. `adjoint_source`: drawn afresh cell by cell.
All inputs are finite; a program needn't handle non-finite values.
Results may differ from a plain program's by a relative error of at most 0.0003.
Values sent between devices are 32-bit elements; how exact they have to be, the bound alone decides.
A program may use at most 128 MiB of HBM per device.

v0:
```python
import math
import jax
import jax.numpy as jnp
from jax import lax
from jax.sharding import PartitionSpec as P

ITERS = 2


def with_halo(block, sides, width):
    for axis, dim in sides:
        count = lax.axis_size(axis)
        forward = [(i, i + 1) for i in range(count - 1)]
        backward = [(target, source) for source, target in forward]
        low = lax.ppermute(
            lax.slice_in_dim(block, block.shape[dim] - width, None, axis=dim), axis, forward
        )
        high = lax.ppermute(lax.slice_in_dim(block, 0, width, axis=dim), axis, backward)
        block = jnp.concatenate([low, block, high], axis=dim)
    return block


def face_coefficients(padded):
    center = padded[1:-1, 1:-1, 1:-1]

    def face(neighbour):
        return jnp.where(neighbour > 0.0, 0.5 * (center + neighbour), center)

    return (
        face(padded[2:, 1:-1, 1:-1]),
        face(padded[:-2, 1:-1, 1:-1]),
        face(padded[1:-1, 2:, 1:-1]),
        face(padded[1:-1, :-2, 1:-1]),
        face(padded[1:-1, 1:-1, 2:]),
        face(padded[1:-1, 1:-1, :-2]),
    )


def apply_operator(rimmed, coeffs):
    padded = jnp.pad(rimmed, ((0, 0), (0, 0), (0, 0), (1, 1)))
    center = padded[:, 1:-1, 1:-1, 1:-1]
    others = (
        padded[:, 2:, 1:-1, 1:-1],
        padded[:, :-2, 1:-1, 1:-1],
        padded[:, 1:-1, 2:, 1:-1],
        padded[:, 1:-1, :-2, 1:-1],
        padded[:, 1:-1, 1:-1, 2:],
        padded[:, 1:-1, 1:-1, :-2],
    )
    total = jnp.zeros(center.shape, jnp.float32)
    for coeff, other in zip(coeffs, others):
        total = total + coeff[None] * (center - other)
    return total


def gram(left, right):
    return jnp.einsum("ixyz,jxyz->ij", left, right, precision=lax.Precision.HIGHEST)


def combine(matrix, block):
    return jnp.einsum("ij,ixyz->jxyz", matrix, block, precision=lax.Precision.HIGHEST)


def small_solve(spd, rhs):
    factor = jnp.linalg.cholesky(spd)
    return jax.scipy.linalg.cho_solve((factor, True), rhs)


def residual_image(residual, coeffs):
    rimmed = with_halo(residual, (("gx", 1), ("gy", 2)), 1)
    return apply_operator(rimmed, coeffs)


def paired_products(residual, image):
    return lax.psum((gram(residual, residual), gram(residual, image)), ("gx", "gy"))


def shards(adjoint_source, conductivity, electrodes):
    rim_sigma = with_halo(conductivity, (("gx", 0), ("gy", 1)), 1)
    coeffs = face_coefficients(jnp.pad(rim_sigma, ((0, 0), (0, 0), (1, 1))))
    cells_x = adjoint_source.shape[1]
    cells_y = adjoint_source.shape[2]
    cells_z = adjoint_source.shape[3]
    total_x = cells_x * lax.axis_size("gx")
    total_y = cells_y * lax.axis_size("gy")
    current = math.sqrt(total_x * total_y * cells_z)
    start_x = lax.axis_index("gx") * cells_x
    start_y = lax.axis_index("gy") * cells_y
    row_x = electrodes // total_y
    row_y = electrodes % total_y
    mark_x = ((start_x + jnp.arange(cells_x, dtype=jnp.int32))[None, :] == row_x[:, None]).astype(
        jnp.float32
    )
    mark_y = ((start_y + jnp.arange(cells_y, dtype=jnp.int32))[None, :] == row_y[:, None]).astype(
        jnp.float32
    )
    spike = current * (mark_x[:, :, None] * mark_y[:, None, :])
    right_side = adjoint_source.at[:, :, :, 0].add(spike)
    solution_field = jnp.zeros_like(right_side)
    residual = right_side
    direction = right_side
    image = residual_image(residual, coeffs)
    norm_now, curvature = paired_products(residual, image)
    along = image
    for step in range(ITERS):
        alpha = small_solve(curvature, norm_now)
        solution_field = solution_field + combine(alpha, direction)
        residual = residual - combine(alpha, along)
        if step + 1 < ITERS:
            image = residual_image(residual, coeffs)
            norm_next, cross = paired_products(residual, image)
            beta = small_solve(norm_now, norm_next)
            weighted = jnp.dot(curvature, beta, precision=lax.Precision.HIGHEST)
            curvature = cross - jnp.dot(beta.T, weighted, precision=lax.Precision.HIGHEST)
            direction = residual + combine(beta, direction)
            along = image + combine(beta, along)
            norm_now = norm_next
    return (solution_field, residual)


def solution(mesh):
    placed = (P(None, "gx", "gy", None), P("gx", "gy", None), P())
    return jax.shard_map(
        shards,
        mesh=mesh,
        in_specs=placed,
        out_specs=(P(None, "gx", "gy", None), P(None, "gx", "gy", None)),
        check_vma=False,
    )
```

profile of v0, /device:TPU:0, one launch (start us, length us, event | category | flops | bytes accessed | tf_op | source)
XLA Modules:
  0.0 340.7 jit_solution(11760287476002612887)
XLA Ops:
  0.6 1.0 fusion.70
  1.6 2.4 collective-permute-start.2
  4.0 1.3 collective-permute-start
  5.3 0.7 and_select_fusion.1
  6.2 4.9 %copy.25 = f32[4,8,64,512]{3,0,2,1:T(4,128)S(1)} copy(f32[4,8,64,512]{3,2,1,0:T(8,128)} %param.8) | data formatting | bytes 8388608 | tf_op args[0]
  11.2 1.9 copy-done.2
  13.4 8.9 %scatter-add.4 = f32[4,8,64,512]{3,0,2,1:T(4,128)} dynamic-update-slice(f32[4,8,64,512]{3,0,2,1:T(4,128)} %copy-done.2, f32[4,8,64,1]{3,0,2,1:T(4,128)S(1)} %slice_add_fusion, s32[]{:T(128)} %constant.100.clone.1, s32[]{:T(128)} %constant.100.clone.1, s32[]{:T(128)} %constant.100.clone.1, s32[]{:T(128)} %constant.100.clone.1) | dynamic-update-slice | bytes 16388 | tf_op jit(solution)/shard_map/scatter-add | solution.py:98
  22.3 1.4 fusion.68
  23.8 1.4 collective-permute-start.1
  25.2 5.8 %collective-permute-start.3 = (f32[4,1,64,512]{3,0,2,1:T(4,128)S(1)}, f32[4,1,64,512]{3,0,2,1:T(4,128)S(1)}, u32[]{:S(2)}, u32[]{:S(2)}) collective-permute-start(f32[4,1,64,512]{3,0,2,1:T(4,128)S(1)} %get-tuple-element.30), channel_id=1, source_target_pairs={{0,4},{4,8},{8,12},{12,16},{16,20},{20,24},{24,28},{1,5},{5,9},{9,... | collective-permute-start | bytes 1572872 | tf_op jit(solution)/shard_map/ppermute | solution.py:15
  31.4 1.3 collective-permute-start.4
  32.7 5.1 %collective-permute-start.6 = (f32[10,1,512]{2,1,0:T(1,128)S(1)}, f32[10,1,512]{2,1,0:T(1,128)S(1)}, u32[]{:S(2)}, u32[]{:S(2)}) collective-permute-start(f32[10,1,512]{2,1,0:T(1,128)S(1)} %get-tuple-element.36), channel_id=1, source_target_pairs={{0,1},{1,2},{2,3},{4,5},{5,6},{6,7},{8,9},{9,10},{10,11},{12,13},{... | collective-permute-start | bytes 61448 | tf_op jit(solution)/shard_map/ppermute | solution.py:15
  37.8 18.0 %convolution_bitcast_fusion.4 = f32[4,4]{0,1:T(4,128)S(1)} fusion(f32[4,8,64,512]{3,0,2,1:T(4,128)S(1)} %copy-done.3), kind=kOutput, calls=%fused_computation.77 | convolution fusion | flops 50331648 | bytes 4194368 | tf_op jit(solution)/shard_map/ixyz,jxyz->ij/dot_general | solution.py:57
  55.8 0.7 select_maximum_fusion.8
  56.6 1.3 collective-permute-start.5
  57.9 4.7 %collective-permute-start.7 = (f32[4,10,1,512]{3,0,2,1:T(4,128)S(1)}, f32[4,10,1,512]{3,0,2,1:T(4,128)S(1)}, u32[]{:S(2)}, u32[]{:S(2)}) collective-permute-start(f32[4,10,1,512]{3,0,2,1:T(4,128)S(1)} %get-tuple-element.26), channel_id=1, source_target_pairs={{0,1},{1,2},{2,3},{4,5},{5,6},{6,7},{8,9},{9,10},{10,11},{12,13},{... | collective-permute-start | bytes 245768 | tf_op jit(solution)/shard_map/ppermute | solution.py:15
  62.7 1.0 multiply_select_fusion.3
  63.7 1.5 collective-permute-done.7
  65.2 11.7 %select_maximum_fusion.4 = f32[4,10,66,514]{3,0,2,1:T(4,128)S(1)} fusion(f32[4,10,1,512]{3,0,2,1:T(4,128)S(1)} %collective-permute-done.5, f32[4,10,1,512]{3,0,2,1:T(4,128)S(1)} %collective-permute-done.7, f32[4,1,64,512]{3,0,2,1:T(4,128)S(1)} %collective-permute-done.1, f32[4,8,64,512]{3,0,2,1:T(4,128)S(1)} %copy-done.3, ...), kind=kLoop, calls=%fused_computation.6 | loop fusion | flops 16283520 | bytes 10834560 | tf_op jit(solution)/shard_map/concatenate | solution.py:19
  77.0 10.1 %fusion.17 = f32[4,8,64,512]{3,0,2,1:T(4,128)S(1)} fusion(f32[4,8,64,512]{3,0,2,1:T(4,128)S(1)} %copy-done.3, f32[4,10,66,514]{3,0,2,1:T(4,128)S(1)} %select_maximum_fusion.4, f32[4,10,1,512]{3,0,2,1:T(4,128)S(1)} %collective-permute-done.7, f32[4,1,64,512]{3,0,2,1:T(4,128)S(1)} %collective-permute-done.1, f32[4,1,64,512]{3,0,2,1:T(4,128)S(1)} %collective-permute-done.3, ...), kind=kLoop, calls=%fused_computation.38 | loop fusion | flops 26214400 | bytes 24281088 | tf_op jit(solution)/shard_map/add | solution.py:52
  87.1 2.0 copy-done.6
  89.1 18.3 %convolution_bitcast_fusion.5 = f32[4,4]{0,1:T(4,128)S(1)} fusion(f32[4,8,64,512]{3,0,2,1:T(4,128)S(1)} %copy-done.3, f32[4,8,64,512]{3,0,2,1:T(4,128)S(1)} %fusion.17), kind=kOutput, calls=%fused_computation.78 | convolution fusion | flops 50331648 | bytes 8388672 | tf_op jit(solution)/shard_map/ixyz,jxyz->ij/dot_general | solution.py:57
  107.3 41.2 %all-reduce.4 = (f32[4,4]{0,1:T(4,128)S(1)}, f32[4,4]{0,1:T(4,128)S(1)}) all-reduce(f32[4,4]{0,1:T(4,128)S(1)} %convolution_bitcast_fusion.4, f32[4,4]{0,1:T(4,128)S(1)} %convolution_bitcast_fusion.5), channel_id=1, replica_groups=mesh['gx'=8,'gy'=4] {'gx','gy'}, use_global_device_ids=true, to_apply=%region_3.5 | all-reduce | flops 32 | bytes 256 | tf_op jit(solution)/shard_map/psum | solution.py:75
  149.2 0.7 compare_reduce_fusion.1
  150.2 0.6 compare_reduce_fusion.2
  152.1 10.1 %convolution_subtract_fusion = f32[4,8,64,512]{3,0,2,1:T(4,128)S(1)} fusion(f32[4,8,64,512]{3,0,2,1:T(4,128)} %scatter-add.4, f32[4,4,1,1]{0,1,3,2:T(4,128)S(1)} %convolution_bitcast_fusion.3, f32[4,8,64,512]{3,0,2,1:T(4,128)} %copy-done.6), kind=kOutput, calls=%fused_computation.67 | convolution fusion | flops 51380224 | bytes 12582976 | tf_op jit(solution)/shard_map/ij,ixyz->jxyz/dot_general | solution.py:61
  162.3 1.3 collective-permute-start.8
  163.6 3.5 %collective-permute-start.9 = (f32[4,1,64,512]{3,0,2,1:T(4,128)S(1)}, f32[4,1,64,512]{3,0,2,1:T(4,128)S(1)}, u32[]{:S(2)}, u32[]{:S(2)}) collective-permute-start(f32[4,1,64,512]{3,0,2,1:T(4,128)S(1)} %get-tuple-element.28), channel_id=1, source_target_pairs={{0,4},{4,8},{8,12},{12,16},{16,20},{20,24},{24,28},{1,5},{5,9},{9,... | collective-permute-start | bytes 1572872 | tf_op jit(solution)/shard_map/ppermute | solution.py:15
  167.1 19.1 %convolution_bitcast_fusion.1 = f32[4,4]{1,0:T(4,128)S(1)} fusion(f32[4,8,64,512]{3,0,2,1:T(4,128)S(1)} %convolution_subtract_fusion), kind=kOutput, calls=%fused_computation.74 | convolution fusion | flops 50331648 | bytes 4194368 | tf_op jit(solution)/shard_map/ixyz,jxyz->ij/dot_general | solution.py:57
  186.3 1.3 collective-permute-start.10
  187.6 4.6 %collective-permute-start.11 = (f32[4,10,1,512]{3,0,2,1:T(4,128)S(1)}, f32[4,10,1,512]{3,0,2,1:T(4,128)S(1)}, u32[]{:S(2)}, u32[]{:S(2)}) collective-permute-start(f32[4,10,1,512]{3,0,2,1:T(4,128)S(1)} %get-tuple-element.24), channel_id=1, source_target_pairs={{0,1},{1,2},{2,3},{4,5},{5,6},{6,7},{8,9},{9,10},{10,11},{12,13},{... | collective-permute-start | bytes 245768 | tf_op jit(solution)/shard_map/ppermute | solution.py:15
  192.2 0.6 fusion.48
  192.8 1.5 collective-permute-done.11
  194.4 11.7 %select_maximum_fusion = f32[4,10,66,514]{3,0,2,1:T(4,128)S(1)} fusion(f32[4,10,1,512]{3,0,2,1:T(4,128)S(1)} %collective-permute-done.10, f32[4,10,1,512]{3,0,2,1:T(4,128)S(1)} %collective-permute-done.11, f32[4,1,64,512]{3,0,2,1:T(4,128)S(1)} %collective-permute-done.8, f32[4,8,64,512]{3,0,2,1:T(4,128)S(1)} %convolution_subtract_fusion, ...), kind=kLoop, calls=%fused_computation.2 | loop fusion | flops 16283520 | bytes 10834560 | tf_op jit(solution)/shard_map/concatenate | solution.py:19
  206.1 10.1 %fusion.2 = f32[4,8,64,512]{3,0,2,1:T(4,128)S(1)} fusion(f32[4,8,64,512]{3,0,2,1:T(4,128)S(1)} %convolution_subtract_fusion, f32[4,10,66,514]{3,0,2,1:T(4,128)S(1)} %select_maximum_fusion, f32[4,10,1,512]{3,0,2,1:T(4,128)S(1)} %collective-permute-done.11, f32[4,1,64,512]{3,0,2,1:T(4,128)S(1)} %collective-permute-done.8, ...), kind=kLoop, calls=%fused_computation.13 | loop fusion | flops 26214400 | bytes 24281088 | tf_op jit(solution)/shard_map/add | solution.py:52
  216.2 2.0 copy-done.7
  218.2 18.3 %convolution_bitcast_fusion.2 = f32[4,4]{0,1:T(4,128)S(1)} fusion(f32[4,8,64,512]{3,0,2,1:T(4,128)S(1)} %convolution_subtract_fusion, f32[4,8,64,512]{3,0,2,1:T(4,128)S(1)} %fusion.2), kind=kOutput, calls=%fused_computation.75 | convolution fusion | flops 50331648 | bytes 8388672 | tf_op jit(solution)/shard_map/ixyz,jxyz->ij/dot_general | solution.py:57
  236.8 41.9 %all-reduce.3 = (f32[4,4]{1,0:T(4,128)S(1)}, f32[4,4]{0,1:T(4,128)S(1)}) all-reduce(f32[4,4]{1,0:T(4,128)S(1)} %convolution_bitcast_fusion.1, f32[4,4]{0,1:T(4,128)S(1)} %convolution_bitcast_fusion.2), channel_id=1, replica_groups=mesh['gx'=8,'gy'=4] {'gx','gy'}, use_global_device_ids=true, to_apply=%region_5.8 | all-reduce | flops 32 | bytes 256 | tf_op jit(solution)/shard_map/psum | solution.py:75
  279.1 11.5 %fusion.60 = f32[4,8,64,512]{3,0,2,1:T(4,128)} fusion(f32[4,8,64,512]{3,0,2,1:T(4,128)} %copy-done.6, f32[4,4]{1,0:T(4,128)S(1)} %fusion.55), kind=kOutput, calls=%fused_computation.122 | convolution fusion | flops 50331648 | bytes 8388672 | tf_op jit(solution)/shard_map/ij,ixyz->jxyz/dot_general | solution.py:61
  290.7 10.3 %fusion.62 = f32[4,8,64,512]{3,0,2,1:T(4,128)} fusion(f32[4,8,64,512]{3,0,2,1:T(4,128)S(1)} %copy-done.4, f32[4,4]{1,0:T(4,128)S(1)} %fusion.55), kind=kOutput, calls=%fused_computation.124 | convolution fusion | flops 50331648 | bytes 8388672 | tf_op jit(solution)/shard_map/ij,ixyz->jxyz/dot_general | solution.py:61
  301.7 0.6 compare_reduce_fusion
  302.4 0.6 fusion.49
  303.8 11.5 %fusion.36 = f32[4,8,64,512]{3,0,2,1:T(4,128)S(1)} fusion(f32[4,8,64,512]{3,0,2,1:T(4,128)} %copy-done, f32[4,4,1,1]{0,1,3,2:T(4,128)S(1)} %convolution_bitcast_fusion, f32[4,8,64,512]{3,0,2,1:T(4,128)} %copy-done.7, f32[4,8,64,512]{3,0,2,1:T(4,128)} %fusion.60), kind=kOutput, calls=%fused_computation.72 | convolution fusion | flops 52428800 | bytes 16777280 | tf_op jit(solution)/shard_map/ij,ixyz->jxyz/dot_general | solution.py:61
  315.3 3.4 %copy.41 = f32[4,8,64,512]{3,2,1,0:T(8,128)} copy(f32[4,8,64,512]{3,0,2,1:T(4,128)S(1)} %fusion.36) | data formatting | bytes 8388608
  318.7 1.5 copy-done.8
  320.3 8.1 %fusion.33 = f32[4,8,64,512]{3,0,2,1:T(4,128)S(1)} fusion(f32[4,4,1,1]{0,1,3,2:T(4,128)S(1)} %convolution_bitcast_fusion, f32[4,8,64,512]{3,0,2,1:T(4,128)S(1)} %copy-done.1, f32[4,8,64,512]{3,0,2,1:T(4,128)S(1)} %copy-done.8), kind=kOutput, calls=%fused_computation.63 | convolution fusion | flops 51380224 | bytes 12582976 | tf_op jit(solution)/shard_map/ij,ixyz->jxyz/dot_general | solution.py:61
  328.4 8.5 %convolution_add_fusion = f32[4,8,64,512]{3,0,2,1:T(4,128)S(1)} fusion(f32[4,8,64,512]{3,0,2,1:T(4,128)S(1)} %fusion.33, f32[4,4,1,1]{0,1,3,2:T(4,128)S(1)} %convolution_bitcast_fusion.3, f32[4,8,64,512]{3,0,2,1:T(4,128)S(1)} %copy-done.5), kind=kOutput, calls=%fused_computation.68 | convolution fusion | flops 51380224 | bytes 12582976 | tf_op jit(solution)/shard_map/ij,ixyz->jxyz/dot_general | solution.py:61
  336.9 3.3 copy.40
  (76 shorter events, 5.8 us)
Async XLA Ops:
  1.6 29.4 %collective-permute-start.2 = (f32[1,64,512]{2,1,0:T(8,128)S(1)}, f32[1,64,512]{2,1,0:T(8,128)S(1)}, u32[]{:S(2)}, u32[]{:S(2)}) collective-permute-start(f32[1,64,512]{2,1,0:T(8,128)S(1)} %get-tuple-element.44), channel_id=1, source_target_pairs={{0,4},{4,8},{8,12},{12,16},{16,20},{20,24},{24,28},{1,5},{5,9},{9,... | collective-permute-start | bytes 393224 | tf_op jit(solution)/shard_map/ppermute | solution.py:15
  4.0 27.0 %collective-permute-start = (f32[1,64,512]{2,1,0:T(8,128)S(1)}, f32[1,64,512]{2,1,0:T(8,128)S(1)}, u32[]{:S(2)}, u32[]{:S(2)}) collective-permute-start(f32[1,64,512]{2,1,0:T(8,128)S(1)} %get-tuple-element.43), channel_id=1, source_target_pairs={{4,0},{8,4},{12,8},{16,12},{20,16},{24,20},{28,24},{5,1},{9,5},{13... | collective-permute-start | bytes 393224 | tf_op jit(solution)/shard_map/ppermute | solution.py:18
  11.1 2.0 copy-start.2
  11.1 19.9 %copy-start.15 = (f32[8,64,512]{2,1,0:T(8,128)S(1)}, f32[8,64,512]{2,1,0:T(8,128)}, u32[]{:S(2)}) copy-start(f32[8,64,512]{2,1,0:T(8,128)} %param.9) | copy-start | bytes 3145732
  22.3 15.5 %copy-start.3 = (f32[4,8,64,512]{3,0,2,1:T(4,128)S(1)}, f32[4,8,64,512]{3,0,2,1:T(4,128)}, u32[]{:S(2)}) copy-start(f32[4,8,64,512]{3,0,2,1:T(4,128)} %scatter-add.4) | copy-start | bytes 12582916
  23.8 32.8 %collective-permute-start.1 = (f32[4,1,64,512]{3,0,2,1:T(4,128)S(1)}, f32[4,1,64,512]{3,0,2,1:T(4,128)S(1)}, u32[]{:S(2)}, u32[]{:S(2)}) collective-permute-start(f32[4,1,64,512]{3,0,2,1:T(4,128)S(1)} %get-tuple-element.31), channel_id=1, source_target_pairs={{4,0},{8,4},{12,8},{16,12},{20,16},{24,20},{28,24},{5,1},{9,5},{13... | collective-permute-start | bytes 1572872 | tf_op jit(solution)/shard_map/ppermute | solution.py:18
  25.2 31.4 %collective-permute-start.3 = (f32[4,1,64,512]{3,0,2,1:T(4,128)S(1)}, f32[4,1,64,512]{3,0,2,1:T(4,128)S(1)}, u32[]{:S(2)}, u32[]{:S(2)}) collective-permute-start(f32[4,1,64,512]{3,0,2,1:T(4,128)S(1)} %get-tuple-element.30), channel_id=1, source_target_pairs={{0,4},{4,8},{8,12},{12,16},{16,20},{20,24},{24,28},{1,5},{5,9},{9,... | collective-permute-start | bytes 1572872 | tf_op jit(solution)/shard_map/ppermute | solution.py:15
  31.4 24.4 %collective-permute-start.4 = (f32[10,1,512]{2,1,0:T(1,128)S(1)}, f32[10,1,512]{2,1,0:T(1,128)S(1)}, u32[]{:S(2)}, u32[]{:S(2)}) collective-permute-start(f32[10,1,512]{2,1,0:T(1,128)S(1)} %get-tuple-element.37), channel_id=1, source_target_pairs={{1,0},{2,1},{3,2},{5,4},{6,5},{7,6},{9,8},{10,9},{11,10},{13,12},{... | collective-permute-start | bytes 61448 | tf_op jit(solution)/shard_map/ppermute | solution.py:18
  32.7 23.1 %collective-permute-start.6 = (f32[10,1,512]{2,1,0:T(1,128)S(1)}, f32[10,1,512]{2,1,0:T(1,128)S(1)}, u32[]{:S(2)}, u32[]{:S(2)}) collective-permute-start(f32[10,1,512]{2,1,0:T(1,128)S(1)} %get-tuple-element.36), channel_id=1, source_target_pairs={{0,1},{1,2},{2,3},{4,5},{5,6},{6,7},{8,9},{9,10},{10,11},{12,13},{... | collective-permute-start | bytes 61448 | tf_op jit(solution)/shard_map/ppermute | solution.py:15
  55.8 6.9 %copy-start.16 = (f32[8,64,512]{2,1,0:T(8,128)S(1)}, f32[8,64,512]{2,1,0:T(8,128)}, u32[]{:S(2)}) copy-start(f32[8,64,512]{2,1,0:T(8,128)} %param.9) | copy-start | bytes 3145732
  56.6 7.1 %collective-permute-start.5 = (f32[4,10,1,512]{3,0,2,1:T(4,128)S(1)}, f32[4,10,1,512]{3,0,2,1:T(4,128)S(1)}, u32[]{:S(2)}, u32[]{:S(2)}) collective-permute-start(f32[4,10,1,512]{3,0,2,1:T(4,128)S(1)} %get-tuple-element.27), channel_id=1, source_target_pairs={{1,0},{2,1},{3,2},{5,4},{6,5},{7,6},{9,8},{10,9},{11,10},{13,12},{... | collective-permute-start | bytes 245768 | tf_op jit(solution)/shard_map/ppermute | solution.py:18
  57.9 7.3 %collective-permute-start.7 = (f32[4,10,1,512]{3,0,2,1:T(4,128)S(1)}, f32[4,10,1,512]{3,0,2,1:T(4,128)S(1)}, u32[]{:S(2)}, u32[]{:S(2)}) collective-permute-start(f32[4,10,1,512]{3,0,2,1:T(4,128)S(1)} %get-tuple-element.26), channel_id=1, source_target_pairs={{0,1},{1,2},{2,3},{4,5},{5,6},{6,7},{8,9},{9,10},{10,11},{12,13},{... | collective-permute-start | bytes 245768 | tf_op jit(solution)/shard_map/ppermute | solution.py:15
  63.7 13.2 %copy-start.9 = (f32[8,64,512]{2,1,0:T(8,128)}, f32[8,64,512]{2,1,0:T(8,128)S(1)}, u32[]{:S(2)}) copy-start(f32[8,64,512]{2,1,0:T(8,128)S(1)} %get-tuple-element.35) | copy-start | bytes 3145732
  63.7 13.2 %copy-start.11 = (f32[8,64,512]{2,1,0:T(8,128)}, f32[8,64,512]{2,1,0:T(8,128)S(1)}, u32[]{:S(2)}) copy-start(f32[8,64,512]{2,1,0:T(8,128)S(1)} %get-tuple-element.41) | copy-start | bytes 3145732
  63.7 13.2 %copy-start.13 = (f32[8,64,512]{2,1,0:T(8,128)}, f32[8,64,512]{2,1,0:T(8,128)S(1)}, u32[]{:S(2)}) copy-start(f32[8,64,512]{2,1,0:T(8,128)S(1)} %get-tuple-element.42) | copy-start | bytes 3145732
  87.1 2.0 copy-start.6
  162.3 54.0 %copy-start = (f32[4,8,64,512]{3,0,2,1:T(4,128)}, f32[4,8,64,512]{3,0,2,1:T(4,128)S(1)}, u32[]{:S(2)}) copy-start(f32[4,8,64,512]{3,0,2,1:T(4,128)S(1)} %convolution_subtract_fusion) | copy-start | bytes 12582916
  162.3 23.9 %collective-permute-start.8 = (f32[4,1,64,512]{3,0,2,1:T(4,128)S(1)}, f32[4,1,64,512]{3,0,2,1:T(4,128)S(1)}, u32[]{:S(2)}, u32[]{:S(2)}) collective-permute-start(f32[4,1,64,512]{3,0,2,1:T(4,128)S(1)} %get-tuple-element.29), channel_id=1, source_target_pairs={{4,0},{8,4},{12,8},{16,12},{20,16},{24,20},{28,24},{5,1},{9,5},{13... | collective-permute-start | bytes 1572872 | tf_op jit(solution)/shard_map/ppermute | solution.py:18
  163.6 22.6 %collective-permute-start.9 = (f32[4,1,64,512]{3,0,2,1:T(4,128)S(1)}, f32[4,1,64,512]{3,0,2,1:T(4,128)S(1)}, u32[]{:S(2)}, u32[]{:S(2)}) collective-permute-start(f32[4,1,64,512]{3,0,2,1:T(4,128)S(1)} %get-tuple-element.28), channel_id=1, source_target_pairs={{0,4},{4,8},{8,12},{12,16},{16,20},{20,24},{24,28},{1,5},{5,9},{9,... | collective-permute-start | bytes 1572872 | tf_op jit(solution)/shard_map/ppermute | solution.py:15
  186.3 6.5 %collective-permute-start.10 = (f32[4,10,1,512]{3,0,2,1:T(4,128)S(1)}, f32[4,10,1,512]{3,0,2,1:T(4,128)S(1)}, u32[]{:S(2)}, u32[]{:S(2)}) collective-permute-start(f32[4,10,1,512]{3,0,2,1:T(4,128)S(1)} %get-tuple-element.25), channel_id=1, source_target_pairs={{1,0},{2,1},{3,2},{5,4},{6,5},{7,6},{9,8},{10,9},{11,10},{13,12},{... | collective-permute-start | bytes 245768 | tf_op jit(solution)/shard_map/ppermute | solution.py:18
  187.6 6.8 %collective-permute-start.11 = (f32[4,10,1,512]{3,0,2,1:T(4,128)S(1)}, f32[4,10,1,512]{3,0,2,1:T(4,128)S(1)}, u32[]{:S(2)}, u32[]{:S(2)}) collective-permute-start(f32[4,10,1,512]{3,0,2,1:T(4,128)S(1)} %get-tuple-element.24), channel_id=1, source_target_pairs={{0,1},{1,2},{2,3},{4,5},{5,6},{6,7},{8,9},{9,10},{10,11},{12,13},{... | collective-permute-start | bytes 245768 | tf_op jit(solution)/shard_map/ppermute | solution.py:15
  192.8 13.3 %copy-start.10 = (f32[8,64,512]{2,1,0:T(8,128)S(1)}, f32[8,64,512]{2,1,0:T(8,128)}, u32[]{:S(2)}) copy-start(f32[8,64,512]{2,1,0:T(8,128)} %copy-done.9) | copy-start | bytes 3145732
  192.8 13.3 %copy-start.12 = (f32[8,64,512]{2,1,0:T(8,128)S(1)}, f32[8,64,512]{2,1,0:T(8,128)}, u32[]{:S(2)}) copy-start(f32[8,64,512]{2,1,0:T(8,128)} %copy-done.11) | copy-start | bytes 3145732
  192.8 13.3 %copy-start.14 = (f32[8,64,512]{2,1,0:T(8,128)S(1)}, f32[8,64,512]{2,1,0:T(8,128)}, u32[]{:S(2)}) copy-start(f32[8,64,512]{2,1,0:T(8,128)} %copy-done.13) | copy-start | bytes 3145732
  216.2 2.0 copy-start.7
  279.1 11.7 %copy-start.4 = (f32[4,8,64,512]{3,0,2,1:T(4,128)S(1)}, f32[4,8,64,512]{3,0,2,1:T(4,128)}, u32[]{:S(2)}) copy-start(f32[4,8,64,512]{3,0,2,1:T(4,128)} %scatter-add.4) | copy-start | bytes 12582916
  315.3 3.4 %copy-start.1 = (f32[4,8,64,512]{3,0,2,1:T(4,128)S(1)}, f32[4,8,64,512]{3,0,2,1:T(4,128)}, u32[]{:S(2)}) copy-start(f32[4,8,64,512]{3,0,2,1:T(4,128)} %copy-done) | copy-start | bytes 12582916
  315.3 5.0 %copy-start.8 = (f32[4,8,64,512]{3,0,2,1:T(4,128)S(1)}, f32[4,8,64,512]{3,0,2,1:T(4,128)}, u32[]{:S(2)}) copy-start(f32[4,8,64,512]{3,0,2,1:T(4,128)} %fusion.62) | copy-start | bytes 12582916
  320.3 8.1 %copy-start.5 = (f32[4,8,64,512]{3,0,2,1:T(4,128)S(1)}, f32[4,8,64,512]{3,0,2,1:T(4,128)}, u32[]{:S(2)}) copy-start(f32[4,8,64,512]{3,0,2,1:T(4,128)} %scatter-add.4) | copy-start | bytes 12582916
where the time goes:
time: 346 us; the launch traced here: 341 us
  matrix products  135 us (39%)
  blocking collectives  83.2 us (24%)
  other arithmetic  52.9 us (15%)
  starting transfers between devices  33.9 us (10%)
  local copies, waits for them, and re-layouts  30.9 us (9%)
    psum x2, blocking collectives, paired_products(): lax.psum((gram(residual, residual), gram(residual, image)), ('gx', 'gy'))  83.2 us
    dot_general x4, matrix products, gram(): jnp.einsum('ixyz,jxyz->ij', left, right, precision=lax.Precision.HIGHEST)  73.6 us
    dot_general x6, matrix products, combine(): jnp.einsum('ij,ixyz->jxyz', matrix, block, precision=lax.Precision.HIGHEST)  60 us
    ppermute x6, starting transfers between devices, with_halo(): lax.ppermute(lax.slice_in_dim(block, block.shape[dim] - width, None, axis...  26 us
    concatenate x5, other arithmetic, with_halo(): block = jnp.concatenate([low, block, high], axis=dim)  24.3 us
    add x2, other arithmetic, apply_operator(): total = total + coeff[None] * (center - other)  20.2 us
    unnamed x38, local copies, waits for them, and re-layouts  19.1 us
    scatter-add x1, local copies, waits for them, and re-layouts, shards(): right_side = adjoint_source.at[:, :, :, 0].add(spike)  8.89 us
  transfers between devices with their start and end apart: 12, of which 2 were waited for; matrix products, arithmetic and copies ran while one was open for 17% of the time, Pallas kernels for 0%

commit v1 on v0

--- a/solution.py
+++ b/solution.py
@@ -5,6 +5,11 @@
 from jax.sharding import PartitionSpec as P
 
 ITERS = 2
+
+
+def _divide_tasks(t0):
+    q_next = lax.psum(t0, "gx")
+    return lax.psum(q_next, "gy")
 
 
 def with_halo(block, sides, width):
@@ -72,7 +77,7 @@
 
 
 def paired_products(residual, image):
-    return lax.psum((gram(residual, residual), gram(residual, image)), ("gx", "gy"))
+    return _divide_tasks((gram(residual, residual), gram(residual, image)))
 
 
 def shards(adjoint_source, conductivity, electrodes):

time: 346 us -> 310 us (0.90)
  blocking collectives: 83.2 us -> 47.4 us
    psum x2 -> x4, blocking collectives: 83.2 us -> 47.4 us  [the longest x2 23.8 us: _divide_tasks(): return lax.psum(q_next, 'gy')]
  transfers between devices with their start and end apart: 12 -> 12, of which waited for: 2 -> 2; matrix products, arithmetic and copies ran while one was open for 17% -> 19% of each run, Pallas kernels for 0% -> 0%
where the time goes in v1:
time: 310 us; the launch traced here: 304 us
  matrix products  135 us (44%)
  other arithmetic  53.1 us (17%)
  blocking collectives  47.4 us (15%)
  starting transfers between devices  33.8 us (11%)
  local copies, waits for them, and re-layouts  30.9 us (10%)
    dot_general x4, matrix products, gram(): jnp.einsum('ixyz,jxyz->ij', left, right, precision=lax.Precision.HIGHEST)  73.6 us
    dot_general x6, matrix products, combine(): jnp.einsum('ij,ixyz->jxyz', matrix, block, precision=lax.Precision.HIGHEST)  59.7 us
    ppermute x6, starting transfers between devices, with_halo(): lax.ppermute(lax.slice_in_dim(block, block.shape[dim] - width, None, axis...  25.9 us
    concatenate x5, other arithmetic, with_halo(): block = jnp.concatenate([low, block, high], axis=dim)  24.3 us
    psum x2, blocking collectives, _divide_tasks(): return lax.psum(q_next, 'gy')  23.8 us
    psum x2, blocking collectives, _divide_tasks(): q_next = lax.psum(t0, 'gx')  23.6 us
    add x2, other arithmetic, apply_operator(): total = total + coeff[None] * (center - other)  20.2 us
    unnamed x38, local copies, waits for them, and re-layouts  19.1 us
  transfers between devices with their start and end apart: 12, of which 2 were waited for; matrix products, arithmetic and copies ran while one was open for 19% of the time, Pallas kernels for 0%

profile of v1, /device:TPU:0, one launch (start us, length us, event | category | flops | bytes accessed | tf_op | source)
XLA Modules:
  0.0 304.5 jit_solution(7033553498119721207)
XLA Ops:
  0.6 1.0 fusion.70
  1.6 2.4 collective-permute-start.2
  4.0 1.3 collective-permute-start
  5.3 0.7 and_select_fusion.1
  6.2 4.9 %copy.25 = f32[4,8,64,512]{3,0,2,1:T(4,128)S(1)} copy(f32[4,8,64,512]{3,2,1,0:T(8,128)} %param.8) | data formatting | bytes 8388608 | tf_op args[0]
  11.2 1.9 copy-done.2
  13.4 8.9 %scatter-add.4 = f32[4,8,64,512]{3,0,2,1:T(4,128)} dynamic-update-slice(f32[4,8,64,512]{3,0,2,1:T(4,128)} %copy-done.2, f32[4,8,64,1]{3,0,2,1:T(4,128)S(1)} %slice_add_fusion, s32[]{:T(128)} %constant.100.clone.1, s32[]{:T(128)} %constant.100.clone.1, s32[]{:T(128)} %constant.100.clone.1, s32[]{:T(128)} %constant.100.clone.1) | dynamic-update-slice | bytes 16388 | tf_op jit(solution)/shard_map/scatter-add | solution.py:103
  22.3 1.4 fusion.68
  23.8 1.4 collective-permute-start.1
  25.2 5.8 %collective-permute-start.3 = (f32[4,1,64,512]{3,0,2,1:T(4,128)S(1)}, f32[4,1,64,512]{3,0,2,1:T(4,128)S(1)}, u32[]{:S(2)}, u32[]{:S(2)}) collective-permute-start(f32[4,1,64,512]{3,0,2,1:T(4,128)S(1)} %get-tuple-element.34), channel_id=1, source_target_pairs={{0,4},{4,8},{8,12},{12,16},{16,20},{20,24},{24,28},{1,5},{5,9},{9,... | collective-permute-start | bytes 1572872 | tf_op jit(solution)/shard_map/ppermute | solution.py:20
  31.4 1.3 collective-permute-start.4
  32.7 5.0 %collective-permute-start.6 = (f32[10,1,512]{2,1,0:T(1,128)S(1)}, f32[10,1,512]{2,1,0:T(1,128)S(1)}, u32[]{:S(2)}, u32[]{:S(2)}) collective-permute-start(f32[10,1,512]{2,1,0:T(1,128)S(1)} %get-tuple-element.40), channel_id=1, source_target_pairs={{0,1},{1,2},{2,3},{4,5},{5,6},{6,7},{8,9},{9,10},{10,11},{12,13},{... | collective-permute-start | bytes 61448 | tf_op jit(solution)/shard_map/ppermute | solution.py:20
  37.8 18.0 %convolution_bitcast_fusion.4 = f32[4,4]{0,1:T(4,128)S(1)} fusion(f32[4,8,64,512]{3,0,2,1:T(4,128)S(1)} %copy-done.3), kind=kOutput, calls=%fused_computation.77 | convolution fusion | flops 50331648 | bytes 4194368 | tf_op jit(solution)/shard_map/ixyz,jxyz->ij/dot_general | solution.py:62
  55.7 0.7 select_maximum_fusion.8
  56.6 1.3 collective-permute-start.5
  57.9 4.7 %collective-permute-start.7 = (f32[4,10,1,512]{3,0,2,1:T(4,128)S(1)}, f32[4,10,1,512]{3,0,2,1:T(4,128)S(1)}, u32[]{:S(2)}, u32[]{:S(2)}) collective-permute-start(f32[4,10,1,512]{3,0,2,1:T(4,128)S(1)} %get-tuple-element.30), channel_id=1, source_target_pairs={{0,1},{1,2},{2,3},{4,5},{5,6},{6,7},{8,9},{9,10},{10,11},{12,13},{... | collective-permute-start | bytes 245768 | tf_op jit(solution)/shard_map/ppermute | solution.py:20
  62.6 1.0 multiply_select_fusion.3
  63.7 1.5 collective-permute-done.7
  65.1 11.7 %select_maximum_fusion.4 = f32[4,10,66,514]{3,0,2,1:T(4,128)S(1)} fusion(f32[4,10,1,512]{3,0,2,1:T(4,128)S(1)} %collective-permute-done.5, f32[4,10,1,512]{3,0,2,1:T(4,128)S(1)} %collective-permute-done.7, f32[4,1,64,512]{3,0,2,1:T(4,128)S(1)} %collective-permute-done.1, f32[4,8,64,512]{3,0,2,1:T(4,128)S(1)} %copy-done.3, ...), kind=kLoop, calls=%fused_computation.6 | loop fusion | flops 16283520 | bytes 10834560 | tf_op jit(solution)/shard_map/concatenate | solution.py:24
  76.9 10.1 %fusion.17 = f32[4,8,64,512]{3,0,2,1:T(4,128)S(1)} fusion(f32[4,8,64,512]{3,0,2,1:T(4,128)S(1)} %copy-done.3, f32[4,10,66,514]{3,0,2,1:T(4,128)S(1)} %select_maximum_fusion.4, f32[4,10,1,512]{3,0,2,1:T(4,128)S(1)} %collective-permute-done.7, f32[4,1,64,512]{3,0,2,1:T(4,128)S(1)} %collective-permute-done.1, f32[4,1,64,512]{3,0,2,1:T(4,128)S(1)} %collective-permute-done.3, ...), kind=kLoop, calls=%fused_computation.38 | loop fusion | flops 26214400 | bytes 24281088 | tf_op jit(solution)/shard_map/add | solution.py:57
  87.0 2.0 copy-done.6
  89.0 18.3 %convolution_bitcast_fusion.5 = f32[4,4]{0,1:T(4,128)S(1)} fusion(f32[4,8,64,512]{3,0,2,1:T(4,128)S(1)} %copy-done.3, f32[4,8,64,512]{3,0,2,1:T(4,128)S(1)} %fusion.17), kind=kOutput, calls=%fused_computation.78 | convolution fusion | flops 50331648 | bytes 8388672 | tf_op jit(solution)/shard_map/ixyz,jxyz->ij/dot_general | solution.py:62
  107.3 11.8 %all-reduce.4 = (f32[4,4]{0,1:T(4,128)S(1)}, f32[4,4]{0,1:T(4,128)S(1)}) all-reduce(f32[4,4]{0,1:T(4,128)S(1)} %convolution_bitcast_fusion.4, f32[4,4]{0,1:T(4,128)S(1)} %convolution_bitcast_fusion.5), channel_id=1, replica_groups=mesh['gx'=8,'gy'=4] {'gx'}, use_global_device_ids=true, to_apply=%region_4.6 | all-reduce | flops 32 | bytes 256 | tf_op jit(solution)/shard_map/psum | solution.py:11
  119.1 12.9 %all-reduce.6 = (f32[4,4]{0,1:T(4,128)S(1)}, f32[4,4]{0,1:T(4,128)S(1)}) all-reduce(f32[4,4]{0,1:T(4,128)S(1)} %get-tuple-element.22, f32[4,4]{0,1:T(4,128)S(1)} %get-tuple-element.23), channel_id=1, replica_groups=mesh['gx'=8,'gy'=4] {'gy'}, use_global_device_ids=true, to_apply=%region_5.7 | all-reduce | flops 32 | bytes 256 | tf_op jit(solution)/shard_map/psum | solution.py:12
  132.5 0.7 compare_reduce_fusion.1
  133.6 0.6 compare_reduce_fusion.2
  135.6 10.1 %convolution_subtract_fusion = f32[4,8,64,512]{3,0,2,1:T(4,128)S(1)} fusion(f32[4,8,64,512]{3,0,2,1:T(4,128)} %scatter-add.4, f32[4,4,1,1]{0,1,3,2:T(4,128)S(1)} %convolution_bitcast_fusion.3, f32[4,8,64,512]{3,0,2,1:T(4,128)} %copy-done.6), kind=kOutput, calls=%fused_computation.67 | convolution fusion | flops 51380224 | bytes 12582976 | tf_op jit(solution)/shard_map/ij,ixyz->jxyz/dot_general | solution.py:66
  145.8 1.3 collective-permute-start.8
  147.1 3.5 %collective-permute-start.9 = (f32[4,1,64,512]{3,0,2,1:T(4,128)S(1)}, f32[4,1,64,512]{3,0,2,1:T(4,128)S(1)}, u32[]{:S(2)}, u32[]{:S(2)}) collective-permute-start(f32[4,1,64,512]{3,0,2,1:T(4,128)S(1)} %get-tuple-element.32), channel_id=1, source_target_pairs={{0,4},{4,8},{8,12},{12,16},{16,20},{20,24},{24,28},{1,5},{5,9},{9,... | collective-permute-start | bytes 1572872 | tf_op jit(solution)/shard_map/ppermute | solution.py:20
  150.6 19.1 %convolution_bitcast_fusion.1 = f32[4,4]{1,0:T(4,128)S(1)} fusion(f32[4,8,64,512]{3,0,2,1:T(4,128)S(1)} %convolution_subtract_fusion), kind=kOutput, calls=%fused_computation.74 | convolution fusion | flops 50331648 | bytes 4194368 | tf_op jit(solution)/shard_map/ixyz,jxyz->ij/dot_general | solution.py:62
  169.8 1.3 collective-permute-start.10
  171.1 4.6 %collective-permute-start.11 = (f32[4,10,1,512]{3,0,2,1:T(4,128)S(1)}, f32[4,10,1,512]{3,0,2,1:T(4,128)S(1)}, u32[]{:S(2)}, u32[]{:S(2)}) collective-permute-start(f32[4,10,1,512]{3,0,2,1:T(4,128)S(1)} %get-tuple-element.28), channel_id=1, source_target_pairs={{0,1},{1,2},{2,3},{4,5},{5,6},{6,7},{8,9},{9,10},{10,11},{12,13},{... | collective-permute-start | bytes 245768 | tf_op jit(solution)/shard_map/ppermute | solution.py:20
  175.6 0.7 fusion.48
  176.4 1.3 collective-permute-done.11
  177.7 11.7 %select_maximum_fusion = f32[4,10,66,514]{3,0,2,1:T(4,128)S(1)} fusion(f32[4,10,1,512]{3,0,2,1:T(4,128)S(1)} %collective-permute-done.10, f32[4,10,1,512]{3,0,2,1:T(4,128)S(1)} %collective-permute-done.11, f32[4,1,64,512]{3,0,2,1:T(4,128)S(1)} %collective-permute-done.8, f32[4,8,64,512]{3,0,2,1:T(4,128)S(1)} %convolution_subtract_fusion, ...), kind=kLoop, calls=%fused_computation.2 | loop fusion | flops 16283520 | bytes 10834560 | tf_op jit(solution)/shard_map/concatenate | solution.py:24
  189.5 10.1 %fusion.2 = f32[4,8,64,512]{3,0,2,1:T(4,128)S(1)} fusion(f32[4,8,64,512]{3,0,2,1:T(4,128)S(1)} %convolution_subtract_fusion, f32[4,10,66,514]{3,0,2,1:T(4,128)S(1)} %select_maximum_fusion, f32[4,10,1,512]{3,0,2,1:T(4,128)S(1)} %collective-permute-done.11, f32[4,1,64,512]{3,0,2,1:T(4,128)S(1)} %collective-permute-done.8, ...), kind=kLoop, calls=%fused_computation.13 | loop fusion | flops 26214400 | bytes 24281088 | tf_op jit(solution)/shard_map/add | solution.py:57
  199.6 2.0 copy-done.7
  201.5 18.3 %convolution_bitcast_fusion.2 = f32[4,4]{0,1:T(4,128)S(1)} fusion(f32[4,8,64,512]{3,0,2,1:T(4,128)S(1)} %convolution_subtract_fusion, f32[4,8,64,512]{3,0,2,1:T(4,128)S(1)} %fusion.2), kind=kOutput, calls=%fused_computation.75 | convolution fusion | flops 50331648 | bytes 8388672 | tf_op jit(solution)/shard_map/ixyz,jxyz->ij/dot_general | solution.py:62
  220.1 11.8 %all-reduce.3 = (f32[4,4]{1,0:T(4,128)S(1)}, f32[4,4]{0,1:T(4,128)S(1)}) all-reduce(f32[4,4]{1,0:T(4,128)S(1)} %convolution_bitcast_fusion.1, f32[4,4]{0,1:T(4,128)S(1)} %convolution_bitcast_fusion.2), channel_id=1, replica_groups=mesh['gx'=8,'gy'=4] {'gx'}, use_global_device_ids=true, to_apply=%region_8.11 | all-reduce | flops 32 | bytes 256 | tf_op jit(solution)/shard_map/psum | solution.py:11
  231.9 10.9 %all-reduce.5 = (f32[4,4]{1,0:T(4,128)S(1)}, f32[4,4]{0,1:T(4,128)S(1)}) all-reduce(f32[4,4]{1,0:T(4,128)S(1)} %get-tuple-element.20, f32[4,4]{0,1:T(4,128)S(1)} %get-tuple-element.21), channel_id=1, replica_groups=mesh['gx'=8,'gy'=4] {'gy'}, use_global_device_ids=true, to_apply=%region_9.12 | all-reduce | flops 32 | bytes 256 | tf_op jit(solution)/shard_map/psum | solution.py:12
  243.2 11.5 %fusion.60 = f32[4,8,64,512]{3,0,2,1:T(4,128)} fusion(f32[4,8,64,512]{3,0,2,1:T(4,128)} %copy-done.6, f32[4,4]{1,0:T(4,128)S(1)} %fusion.55), kind=kOutput, calls=%fused_computation.122 | convolution fusion | flops 50331648 | bytes 8388672 | tf_op jit(solution)/shard_map/ij,ixyz->jxyz/dot_general | solution.py:66
  254.9 10.3 %fusion.62 = f32[4,8,64,512]{3,0,2,1:T(4,128)} fusion(f32[4,8,64,512]{3,0,2,1:T(4,128)S(1)} %copy-done.4, f32[4,4]{1,0:T(4,128)S(1)} %fusion.55), kind=kOutput, calls=%fused_computation.124 | convolution fusion | flops 50331648 | bytes 8388672 | tf_op jit(solution)/shard_map/ij,ixyz->jxyz/dot_general | solution.py:66
  267.9 11.5 %fusion.36 = f32[4,8,64,512]{3,0,2,1:T(4,128)S(1)} fusion(f32[4,8,64,512]{3,0,2,1:T(4,128)} %copy-done, f32[4,4,1,1]{0,1,3,2:T(4,128)S(1)} %convolution_bitcast_fusion, f32[4,8,64,512]{3,0,2,1:T(4,128)} %copy-done.7, f32[4,8,64,512]{3,0,2,1:T(4,128)} %fusion.60), kind=kOutput, calls=%fused_computation.72 | convolution fusion | flops 52428800 | bytes 16777280 | tf_op jit(solution)/shard_map/ij,ixyz->jxyz/dot_general | solution.py:66
  279.4 3.4 %copy.41 = f32[4,8,64,512]{3,2,1,0:T(8,128)} copy(f32[4,8,64,512]{3,0,2,1:T(4,128)S(1)} %fusion.36) | data formatting | bytes 8388608
  282.8 1.5 copy-done.8
  284.4 8.1 %fusion.33 = f32[4,8,64,512]{3,0,2,1:T(4,128)S(1)} fusion(f32[4,4,1,1]{0,1,3,2:T(4,128)S(1)} %convolution_bitcast_fusion, f32[4,8,64,512]{3,0,2,1:T(4,128)S(1)} %copy-done.1, f32[4,8,64,512]{3,0,2,1:T(4,128)S(1)} %copy-done.8), kind=kOutput, calls=%fused_computation.63 | convolution fusion | flops 51380224 | bytes 12582976 | tf_op jit(solution)/shard_map/ij,ixyz->jxyz/dot_general | solution.py:66
  292.5 8.2 %convolution_add_fusion = f32[4,8,64,512]{3,0,2,1:T(4,128)S(1)} fusion(f32[4,8,64,512]{3,0,2,1:T(4,128)S(1)} %fusion.33, f32[4,4,1,1]{0,1,3,2:T(4,128)S(1)} %convolution_bitcast_fusion.3, f32[4,8,64,512]{3,0,2,1:T(4,128)S(1)} %copy-done.5), kind=kOutput, calls=%fused_computation.68 | convolution fusion | flops 51380224 | bytes 12582976 | tf_op jit(solution)/shard_map/ij,ixyz->jxyz/dot_general | solution.py:66
  300.7 3.3 %copy.40 = f32[4,8,64,512]{3,2,1,0:T(8,128)} copy(f32[4,8,64,512]{3,0,2,1:T(4,128)S(1)} %convolution_add_fusion) | data formatting | bytes 8388608
  (78 shorter events, 7.1 us)
Async XLA Ops:
  1.6 29.4 %collective-permute-start.2 = (f32[1,64,512]{2,1,0:T(8,128)S(1)}, f32[1,64,512]{2,1,0:T(8,128)S(1)}, u32[]{:S(2)}, u32[]{:S(2)}) collective-permute-start(f32[1,64,512]{2,1,0:T(8,128)S(1)} %get-tuple-element.48), channel_id=1, source_target_pairs={{0,4},{4,8},{8,12},{12,16},{16,20},{20,24},{24,28},{1,5},{5,9},{9,... | collective-permute-start | bytes 393224 | tf_op jit(solution)/shard_map/ppermute | solution.py:20
  4.0 27.0 %collective-permute-start = (f32[1,64,512]{2,1,0:T(8,128)S(1)}, f32[1,64,512]{2,1,0:T(8,128)S(1)}, u32[]{:S(2)}, u32[]{:S(2)}) collective-permute-start(f32[1,64,512]{2,1,0:T(8,128)S(1)} %get-tuple-element.47), channel_id=1, source_target_pairs={{4,0},{8,4},{12,8},{16,12},{20,16},{24,20},{28,24},{5,1},{9,5},{13... | collective-permute-start | bytes 393224 | tf_op jit(solution)/shard_map/ppermute | solution.py:23
  11.1 2.0 copy-start.2
  11.1 19.9 %copy-start.15 = (f32[8,64,512]{2,1,0:T(8,128)S(1)}, f32[8,64,512]{2,1,0:T(8,128)}, u32[]{:S(2)}) copy-start(f32[8,64,512]{2,1,0:T(8,128)} %param.9) | copy-start | bytes 3145732
  22.3 15.4 %copy-start.3 = (f32[4,8,64,512]{3,0,2,1:T(4,128)S(1)}, f32[4,8,64,512]{3,0,2,1:T(4,128)}, u32[]{:S(2)}) copy-start(f32[4,8,64,512]{3,0,2,1:T(4,128)} %scatter-add.4) | copy-start | bytes 12582916
  23.8 32.7 %collective-permute-start.1 = (f32[4,1,64,512]{3,0,2,1:T(4,128)S(1)}, f32[4,1,64,512]{3,0,2,1:T(4,128)S(1)}, u32[]{:S(2)}, u32[]{:S(2)}) collective-permute-start(f32[4,1,64,512]{3,0,2,1:T(4,128)S(1)} %get-tuple-element.35), channel_id=1, source_target_pairs={{4,0},{8,4},{12,8},{16,12},{20,16},{24,20},{28,24},{5,1},{9,5},{13... | collective-permute-start | bytes 1572872 | tf_op jit(solution)/shard_map/ppermute | solution.py:23
  25.2 31.3 %collective-permute-start.3 = (f32[4,1,64,512]{3,0,2,1:T(4,128)S(1)}, f32[4,1,64,512]{3,0,2,1:T(4,128)S(1)}, u32[]{:S(2)}, u32[]{:S(2)}) collective-permute-start(f32[4,1,64,512]{3,0,2,1:T(4,128)S(1)} %get-tuple-element.34), channel_id=1, source_target_pairs={{0,4},{4,8},{8,12},{12,16},{16,20},{20,24},{24,28},{1,5},{5,9},{9,... | collective-permute-start | bytes 1572872 | tf_op jit(solution)/shard_map/ppermute | solution.py:20
  31.4 24.3 %collective-permute-start.4 = (f32[10,1,512]{2,1,0:T(1,128)S(1)}, f32[10,1,512]{2,1,0:T(1,128)S(1)}, u32[]{:S(2)}, u32[]{:S(2)}) collective-permute-start(f32[10,1,512]{2,1,0:T(1,128)S(1)} %get-tuple-element.41), channel_id=1, source_target_pairs={{1,0},{2,1},{3,2},{5,4},{6,5},{7,6},{9,8},{10,9},{11,10},{13,12},{... | collective-permute-start | bytes 61448 | tf_op jit(solution)/shard_map/ppermute | solution.py:23
  32.7 23.0 %collective-permute-start.6 = (f32[10,1,512]{2,1,0:T(1,128)S(1)}, f32[10,1,512]{2,1,0:T(1,128)S(1)}, u32[]{:S(2)}, u32[]{:S(2)}) collective-permute-start(f32[10,1,512]{2,1,0:T(1,128)S(1)} %get-tuple-element.40), channel_id=1, source_target_pairs={{0,1},{1,2},{2,3},{4,5},{5,6},{6,7},{8,9},{9,10},{10,11},{12,13},{... | collective-permute-start | bytes 61448 | tf_op jit(solution)/shard_map/ppermute | solution.py:20
  55.7 6.9 %copy-start.16 = (f32[8,64,512]{2,1,0:T(8,128)S(1)}, f32[8,64,512]{2,1,0:T(8,128)}, u32[]{:S(2)}) copy-start(f32[8,64,512]{2,1,0:T(8,128)} %param.9) | copy-start | bytes 3145732
  56.6 7.1 %collective-permute-start.5 = (f32[4,10,1,512]{3,0,2,1:T(4,128)S(1)}, f32[4,10,1,512]{3,0,2,1:T(4,128)S(1)}, u32[]{:S(2)}, u32[]{:S(2)}) collective-permute-start(f32[4,10,1,512]{3,0,2,1:T(4,128)S(1)} %get-tuple-element.31), channel_id=1, source_target_pairs={{1,0},{2,1},{3,2},{5,4},{6,5},{7,6},{9,8},{10,9},{11,10},{13,12},{... | collective-permute-start | bytes 245768 | tf_op jit(solution)/shard_map/ppermute | solution.py:23
  57.9 7.3 %collective-permute-start.7 = (f32[4,10,1,512]{3,0,2,1:T(4,128)S(1)}, f32[4,10,1,512]{3,0,2,1:T(4,128)S(1)}, u32[]{:S(2)}, u32[]{:S(2)}) collective-permute-start(f32[4,10,1,512]{3,0,2,1:T(4,128)S(1)} %get-tuple-element.30), channel_id=1, source_target_pairs={{0,1},{1,2},{2,3},{4,5},{5,6},{6,7},{8,9},{9,10},{10,11},{12,13},{... | collective-permute-start | bytes 245768 | tf_op jit(solution)/shard_map/ppermute | solution.py:20
  63.6 13.2 %copy-start.9 = (f32[8,64,512]{2,1,0:T(8,128)}, f32[8,64,512]{2,1,0:T(8,128)S(1)}, u32[]{:S(2)}) copy-start(f32[8,64,512]{2,1,0:T(8,128)S(1)} %get-tuple-element.39) | copy-start | bytes 3145732
  63.6 13.2 %copy-start.11 = (f32[8,64,512]{2,1,0:T(8,128)}, f32[8,64,512]{2,1,0:T(8,128)S(1)}, u32[]{:S(2)}) copy-start(f32[8,64,512]{2,1,0:T(8,128)S(1)} %get-tuple-element.45) | copy-start | bytes 3145732
  63.7 13.2 %copy-start.13 = (f32[8,64,512]{2,1,0:T(8,128)}, f32[8,64,512]{2,1,0:T(8,128)S(1)}, u32[]{:S(2)}) copy-start(f32[8,64,512]{2,1,0:T(8,128)S(1)} %get-tuple-element.46) | copy-start | bytes 3145732
  87.0 2.0 copy-start.6
  145.7 53.8 %copy-start = (f32[4,8,64,512]{3,0,2,1:T(4,128)}, f32[4,8,64,512]{3,0,2,1:T(4,128)S(1)}, u32[]{:S(2)}) copy-start(f32[4,8,64,512]{3,0,2,1:T(4,128)S(1)} %convolution_subtract_fusion) | copy-start | bytes 12582916
  145.8 23.9 %collective-permute-start.8 = (f32[4,1,64,512]{3,0,2,1:T(4,128)S(1)}, f32[4,1,64,512]{3,0,2,1:T(4,128)S(1)}, u32[]{:S(2)}, u32[]{:S(2)}) collective-permute-start(f32[4,1,64,512]{3,0,2,1:T(4,128)S(1)} %get-tuple-element.33), channel_id=1, source_target_pairs={{4,0},{8,4},{12,8},{16,12},{20,16},{24,20},{28,24},{5,1},{9,5},{13... | collective-permute-start | bytes 1572872 | tf_op jit(solution)/shard_map/ppermute | solution.py:23
  147.1 22.6 %collective-permute-start.9 = (f32[4,1,64,512]{3,0,2,1:T(4,128)S(1)}, f32[4,1,64,512]{3,0,2,1:T(4,128)S(1)}, u32[]{:S(2)}, u32[]{:S(2)}) collective-permute-start(f32[4,1,64,512]{3,0,2,1:T(4,128)S(1)} %get-tuple-element.32), channel_id=1, source_target_pairs={{0,4},{4,8},{8,12},{12,16},{16,20},{20,24},{24,28},{1,5},{5,9},{9,... | collective-permute-start | bytes 1572872 | tf_op jit(solution)/shard_map/ppermute | solution.py:20
  169.8 6.6 %collective-permute-start.10 = (f32[4,10,1,512]{3,0,2,1:T(4,128)S(1)}, f32[4,10,1,512]{3,0,2,1:T(4,128)S(1)}, u32[]{:S(2)}, u32[]{:S(2)}) collective-permute-start(f32[4,10,1,512]{3,0,2,1:T(4,128)S(1)} %get-tuple-element.29), channel_id=1, source_target_pairs={{1,0},{2,1},{3,2},{5,4},{6,5},{7,6},{9,8},{10,9},{11,10},{13,12},{... | collective-permute-start | bytes 245768 | tf_op jit(solution)/shard_map/ppermute | solution.py:23
  171.1 6.6 %collective-permute-start.11 = (f32[4,10,1,512]{3,0,2,1:T(4,128)S(1)}, f32[4,10,1,512]{3,0,2,1:T(4,128)S(1)}, u32[]{:S(2)}, u32[]{:S(2)}) collective-permute-start(f32[4,10,1,512]{3,0,2,1:T(4,128)S(1)} %get-tuple-element.28), channel_id=1, source_target_pairs={{0,1},{1,2},{2,3},{4,5},{5,6},{6,7},{8,9},{9,10},{10,11},{12,13},{... | collective-permute-start | bytes 245768 | tf_op jit(solution)/shard_map/ppermute | solution.py:20
  176.3 13.1 %copy-start.10 = (f32[8,64,512]{2,1,0:T(8,128)S(1)}, f32[8,64,512]{2,1,0:T(8,128)}, u32[]{:S(2)}) copy-start(f32[8,64,512]{2,1,0:T(8,128)} %copy-done.9) | copy-start | bytes 3145732
  176.3 13.1 %copy-start.12 = (f32[8,64,512]{2,1,0:T(8,128)S(1)}, f32[8,64,512]{2,1,0:T(8,128)}, u32[]{:S(2)}) copy-start(f32[8,64,512]{2,1,0:T(8,128)} %copy-done.11) | copy-start | bytes 3145732
  176.4 13.1 %copy-start.14 = (f32[8,64,512]{2,1,0:T(8,128)S(1)}, f32[8,64,512]{2,1,0:T(8,128)}, u32[]{:S(2)}) copy-start(f32[8,64,512]{2,1,0:T(8,128)} %copy-done.13) | copy-start | bytes 3145732
  199.5 2.0 copy-start.7
  243.2 11.7 %copy-start.4 = (f32[4,8,64,512]{3,0,2,1:T(4,128)S(1)}, f32[4,8,64,512]{3,0,2,1:T(4,128)}, u32[]{:S(2)}) copy-start(f32[4,8,64,512]{3,0,2,1:T(4,128)} %scatter-add.4) | copy-start | bytes 12582916
  279.4 3.4 %copy-start.1 = (f32[4,8,64,512]{3,0,2,1:T(4,128)S(1)}, f32[4,8,64,512]{3,0,2,1:T(4,128)}, u32[]{:S(2)}) copy-start(f32[4,8,64,512]{3,0,2,1:T(4,128)} %copy-done) | copy-start | bytes 12582916
  279.4 5.0 %copy-start.8 = (f32[4,8,64,512]{3,0,2,1:T(4,128)S(1)}, f32[4,8,64,512]{3,0,2,1:T(4,128)}, u32[]{:S(2)}) copy-start(f32[4,8,64,512]{3,0,2,1:T(4,128)} %fusion.62) | copy-start | bytes 12582916
  284.4 8.1 %copy-start.5 = (f32[4,8,64,512]{3,0,2,1:T(4,128)S(1)}, f32[4,8,64,512]{3,0,2,1:T(4,128)}, u32[]{:S(2)}) copy-start(f32[4,8,64,512]{3,0,2,1:T(4,128)} %scatter-add.4) | copy-start | bytes 12582916
